TPU v7x, 512 devices: a whole 4x4x16 slice. The times are simulated.
512 devices in a mesh: bond: 32 (over z_lo, x, core), leg: 16 (over z_hi, y).
Axes of the slice: x: 4, y: 4, z: 16 (z_hi: 4, z_lo: 4; z = z_hi * 4 + z_lo), core: 2. Of those that a mesh axis runs over, the one named last changes fastest.
Arguments:
- amplitudes: float32 [2, 1024, 262144], P(None, 'bond', 'leg'), may hold values from -6 to 6
- vectors: float32 [64, 262144], P(None, ('leg', 'bond')), may hold values from -0.01171875 to 0.01171875
- row_map: float32 [64, 4096], P('leg'), may hold values from -0.09375 to 0.09375
- col_map: float32 [64, 4096], P('bond'), may hold values from -0.09375 to 0.09375
Outputs:
- coarse: float32 [2, 8, 64, 64], P(None, None, 'leg', 'bond')
All inputs are finite; a program needn't handle non-finite values.
Results may differ from a plain program's by a relative error of at most 0.00014.
Values sent between devices are 32-bit elements; how exact they have to be, the bound alone decides.
A program may use at most 64 MiB of HBM per device.

v0:
```python
import jax
import jax.numpy as jnp
from jax import lax
from jax.sharding import PartitionSpec as P


def coarsen(slab, row_maps, col_maps):
    highest = lax.Precision.HIGHEST
    even = slab[:, 0::2]
    odd = slab[:, 1::2]
    inner = jnp.einsum("ztjc,qcd->ztqjd", even, col_maps, precision=highest)
    real_part = jnp.einsum("tqjd,tkd->tqjk", inner[0], odd[0], precision=highest) - jnp.einsum(
        "tqjd,tkd->tqjk", inner[1], odd[1], precision=highest
    )
    imag_part = jnp.einsum("tqjd,tkd->tqjk", inner[0], odd[1], precision=highest) + jnp.einsum(
        "tqjd,tkd->tqjk", inner[1], odd[0], precision=highest
    )
    paired = jnp.stack([real_part, imag_part])
    return jnp.einsum("pjk,ztqjk->ztpq", row_maps, paired, precision=highest)


def local(amplitudes, vectors, row_map, col_map):
    highest = lax.Precision.HIGHEST
    bond_dim = vectors.shape[0]
    partial_proj = jnp.einsum(
        "jk,zrk->zjr",
        lax.all_gather(vectors, "bond", axis=1, tiled=True),
        amplitudes,
        precision=highest,
    )
    summed = lax.psum(partial_proj, "leg")
    projected = lax.all_gather(summed, "bond", axis=2, tiled=True)
    slab_count = projected.shape[2] // bond_dim
    slab = projected.reshape(2, bond_dim, slab_count, bond_dim).transpose(0, 2, 1, 3)
    row_maps = row_map.reshape(row_map.shape[0], bond_dim, bond_dim)
    col_maps = col_map.reshape(col_map.shape[0], bond_dim, bond_dim)
    return coarsen(slab, row_maps, col_maps)


def solution(mesh):
    return jax.shard_map(
        local,
        mesh=mesh,
        in_specs=(
            P(None, "bond", "leg"),
            P(None, ("leg", "bond")),
            P("leg", None),
            P("bond", None),
        ),
        out_specs=P(None, None, "leg", "bond"),
        check_vma=False,
    )
```

profile of v0, /device:TPU:1, one launch (start us, length us, event | category | flops | bytes accessed | tf_op | source)
XLA Modules:
  0.0 250.0 jit_solution(4915478160259681730)
XLA Ops:
  6.5 0.0 all-gather.2.cloned.1.call-start
  6.5 0.7 all-gather.2.cloned.1.call-update
  7.3 0.9 reshape.14
  8.1 1.0 reshape.11
  9.1 73.8 %all-gather.2.cloned.1.call-done = f32[64,16384]{1,0:T(8,128)} async-done(((f32[64,512]{1,0:T(8,128)}), f32[64,16384]{1,0:T(8,128)}) %all-gather.2.cloned.1.call-update) | async-done | bytes 4194320 | tf_op jit(solution)/shard_map/all_gather | solution.py:27
  82.8 6.9 %fusion.4 = f32[2,64,32]{1,2,0:T(8,128)S(1)} fusion(f32[2,32,16384]{2,1,0:T(8,128)} %param.4, f32[64,16384]{1,0:T(8,128)} %all-gather.2.cloned.1.call-done), kind=kOutput, calls=%fused_computation.7 | convolution fusion | flops 805306368 | bytes 8404992 | tf_op jit(solution)/shard_map/jk,zrk->zjr/dot_general | solution.py:25
  89.8 84.2 %psum.7 = f32[2,64,32]{1,2,0:T(8,128)S(1)} all-reduce(f32[2,64,32]{1,2,0:T(8,128)S(1)} %fusion.4), channel_id=1, replica_groups=mesh['bond'=32,'leg'=16] {'leg'}, use_global_device_ids=true, to_apply=%region_0.0 | all-reduce | flops 4096 | bytes 32768 | tf_op jit(solution)/shard_map/psum | solution.py:31
  174.0 57.6 %all_gather.7 = f32[2,64,1024]{1,2,0:T(8,128)S(1)} all-gather(f32[2,64,32]{1,2,0:T(8,128)S(1)} %psum.7), channel_id=1, replica_groups=mesh['bond'=32,'leg'=16] {'bond'}, dimensions={2}, use_global_device_ids=true | all-gather | bytes 540672 | tf_op jit(solution)/shard_map/all_gather | solution.py:32
  231.5 0.3 copy.5
  231.9 1.0 convolution_bitcast_fusion
  232.9 0.6 fusion.10
  233.5 0.6 fusion.11
  234.1 0.6 fusion.2
  234.8 0.6 fusion.3
  235.4 0.1 pad_maximum_fusion
  235.5 7.0 %convolution_bitcast_fusion.1 = f32[2,8,4,2]{1,2,3,0:T(4,128)S(1)} fusion(f32[2,8,2,64,64]{4,3,2,1,0:T(8,128)S(1)} %pad_maximum_fusion, f32[4,64,64,1,1]{2,1,0,4,3:T(8,128)S(1)} %bitcast.55), kind=kOutput, calls=%fused_computation.8 | convolution fusion | flops 6291456 | bytes 590336 | tf_op jit(solution)/shard_map/pjk,ztqjk->ztpq/dot_general | solution.py:19
  242.5 0.6 copy.8
  (1 shorter events, 0.0 us)
Async XLA Ops:
  6.5 76.3 %all-gather.2.cloned.1.call-start = ((), (), s32[]{:S(2)}) async-start(), calls=%async_computation | async-start | bytes 4325376 | tf_op jit(solution)/shard_map/all_gather | solution.py:27
Sparse Core Ops, SparseCore 0:
  9.5 73.3 all-gather.1
where the time goes:
time: 250 us
  blocking collectives  142 us (57%)
  waiting for transfers between devices  74.5 us (30%)
  matrix products  17.4 us (7%)
  between operations  13.5 us (5%)
  local copies, waits for them, and re-layouts  2.82 us (1%)
    psum x1, blocking collectives, local(): summed = lax.psum(partial_proj, 'leg')  84.2 us
    all_gather x1, waiting for transfers between devices, local(): lax.all_gather(vectors, 'bond', axis=1, tiled=True)  73.8 us
    all_gather x1, blocking collectives, local(): projected = lax.all_gather(summed, 'bond', axis=2, tiled=True)  57.6 us
    dot_general x1, matrix products, coarsen(): return jnp.einsum('pjk,ztqjk->ztpq', row_maps, paired, precision=highest)  6.99 us
    dot_general x1, matrix products, local(): jnp.einsum('jk,zrk->zjr', lax.all_gather(vectors, 'bond', axis=1, tiled=T...  6.94 us
  transfers between devices with their start and end apart: 1, of which 1 were waited for; matrix products, arithmetic and copies ran while one was open for 1% of the time, Pallas kernels for 0%

commit v1 on v0

--- a/solution.py
+++ b/solution.py
@@ -1,7 +1,18 @@
+import functools
 import jax
 import jax.numpy as jnp
 from jax import lax
 from jax.sharding import PartitionSpec as P
+
+
+def loads_write(arr, comm_axis):
+    raw_out = lax.axis_size(comm_axis)
+    carry_in = jnp.stack(raw_out * [arr], 0)
+    last = lax.all_to_all(carry_in, axis_name=comm_axis, split_axis=0, concat_axis=0)
+    return jnp.concatenate(last, 1)
+
+
+wrap_the_tables = functools.partial(loads_write, comm_axis="bond")
 
 
 def coarsen(slab, row_maps, col_maps):
@@ -23,10 +34,7 @@
     highest = lax.Precision.HIGHEST
     bond_dim = vectors.shape[0]
     partial_proj = jnp.einsum(
-        "jk,zrk->zjr",
-        lax.all_gather(vectors, "bond", axis=1, tiled=True),
-        amplitudes,
-        precision=highest,
+        "jk,zrk->zjr", wrap_the_tables(vectors), amplitudes, precision=highest
     )
     summed = lax.psum(partial_proj, "leg")
     projected = lax.all_gather(summed, "bond", axis=2, tiled=True)

time: 250 us -> 284 us (1.14)
  waiting for transfers between devices: 74.5 us -> 92.9 us
  between operations: 13.5 us -> 0.09 us
  local copies, waits for them, and re-layouts: 2.82 us -> 16.1 us
  starting transfers between devices: 0.01 us -> 11.4 us
  blocking collectives: 142 us -> 145 us
    all_to_all x0 -> x1, waiting for transfers between devices: none -> 92.9 us  [loads_write(): lax.all_to_all(carry_in, axis_name=comm_axis, split_axis=0, concat_axis=0)]
    all_gather x1 -> x0, waiting for transfers between devices: 73.8 us -> none  [local(): lax.all_gather(vectors, 'bond', axis=1, tiled=True)]
    reshape x0 -> x2, local copies, waits for them, and re-layouts: none -> 11.5 us  [loads_write(): return jnp.concatenate(last, 1)]
    all_to_all x0 -> x1, starting transfers between devices: none -> 11.4 us  [loads_write(): lax.all_to_all(carry_in, axis_name=comm_axis, split_axis=0, concat_axis=0)]
    another operation x0 -> x1, local copies, waits for them, and re-layouts: none -> 3.39 us  [loads_write(): carry_in = jnp.stack(raw_out * [arr], 0)]
  transfers between devices with their start and end apart: 1 -> 1, of which waited for: 1 -> 1; matrix products, arithmetic and copies ran while one was open for 1% -> 0% of each run, Pallas kernels for 0% -> 0%
where the time goes in v1:
time: 284 us; the launch traced here: 283 us
  blocking collectives  145 us (51%)
  waiting for transfers between devices  92.9 us (33%)
  matrix products  17.4 us (6%)
  local copies, waits for them, and re-layouts  16.1 us (6%)
  starting transfers between devices  11.4 us (4%)
    all_to_all x1, waiting for transfers between devices, loads_write(): lax.all_to_all(carry_in, axis_name=comm_axis, split_axis=0, concat_axis=0)  92.9 us
    psum x1, blocking collectives, local(): summed = lax.psum(partial_proj, 'leg')  86.2 us
    all_gather x1, blocking collectives, local(): projected = lax.all_gather(summed, 'bond', axis=2, tiled=True)  59 us
    reshape x2, local copies, waits for them, and re-layouts, loads_write(): return jnp.concatenate(last, 1)  11.5 us
    all_to_all x1, starting transfers between devices, loads_write(): lax.all_to_all(carry_in, axis_name=comm_axis, split_axis=0, concat_axis=0)  11.4 us
    dot_general x1, matrix products, coarsen(): return jnp.einsum('pjk,ztqjk->ztpq', row_maps, paired, precision=highest)  6.99 us
    dot_general x1, matrix products, local(): jnp.einsum('jk,zrk->zjr', wrap_the_tables(vectors), amplitudes, precision...  6.93 us
  transfers between devices with their start and end apart: 1, of which 1 were waited for; matrix products, arithmetic and copies ran while one was open for 0% of the time, Pallas kernels for 0%

profile of v1, /device:TPU:1, one launch (start us, length us, event | category | flops | bytes accessed | tf_op | source)
XLA Modules:
  0.0 283.3 jit_solution(16803243802647067774)
XLA Ops:
  0.0 3.4 %stack.8 = f32[32,64,512]{2,1,0:T(8,128)} broadcast(f32[64,512]{1,0:T(8,128)} %param.5), dimensions={1,2} | broadcast | bytes 4325376 | tf_op jit(solution)/shard_map/stack | solution.py:10
  3.4 0.0 copy-start.1
  3.4 0.0 copy-start
  3.4 11.4 %all-to-all-start = ((f32[32,64,512]{2,1,0:T(8,128)}), f32[32,64,512]{2,1,0:T(8,128)}, u32[]{:S(2)}, u32[]{:S(2)}) async-start(f32[32,64,512]{2,1,0:T(8,128)} %stack.8), calls=%async_computation | async-start | bytes 8388608 | tf_op jit(solution)/shard_map/all_to_all | solution.py:11
  14.8 0.0 copy-done.1
  14.8 0.1 reshape.24
  14.9 0.0 copy-done
  14.9 0.1 reshape.21
  15.0 92.9 %all-to-all-done = f32[32,64,512]{2,1,0:T(8,128)} async-done(((f32[32,64,512]{2,1,0:T(8,128)}), f32[32,64,512]{2,1,0:T(8,128)}, u32[]{:S(2)}, u32[]{:S(2)}) %all-to-all-start) | async-done | bytes 4194336 | tf_op jit(solution)/shard_map/all_to_all | solution.py:11
  108.0 6.6 %copy.9 = f32[64,32,512]{2,1,0:T(8,128)} copy(f32[64,32,512]{2,0,1:T(8,128)} %bitcast) | data formatting | bytes 8388608 | tf_op jit(solution)/shard_map/reshape | solution.py:12
  114.5 4.9 %reshape.22 = f32[64,16384,1]{1,0,2:T(8,128)} reshape(f32[64,32,512]{2,1,0:T(8,128)} %copy.9) | data formatting | bytes 8388608 | tf_op jit(solution)/shard_map/reshape | solution.py:12
  119.5 6.9 %convolution_bitcast_fusion.1 = f32[2,64,32]{1,2,0:T(8,128)S(1)} fusion(f32[2,32,16384]{2,1,0:T(8,128)} %param.4, f32[64,16384,1]{1,0,2:T(8,128)} %reshape.22), kind=kOutput, calls=%fused_computation.5 | convolution fusion | flops 805306368 | bytes 8404992 | tf_op jit(solution)/shard_map/jk,zrk->zjr/dot_general | solution.py:36
  126.4 86.2 %psum.7 = f32[2,64,32]{1,2,0:T(8,128)S(1)} all-reduce(f32[2,64,32]{1,2,0:T(8,128)S(1)} %convolution_bitcast_fusion.1), channel_id=1, replica_groups=mesh['bond'=32,'leg'=16] {'leg'}, use_global_device_ids=true, to_apply=%region_0.0 | all-reduce | flops 4096 | bytes 32768 | tf_op jit(solution)/shard_map/psum | solution.py:39
  212.7 59.0 %all_gather.3 = f32[2,64,1024]{1,2,0:T(8,128)S(1)} all-gather(f32[2,64,32]{1,2,0:T(8,128)S(1)} %psum.7), channel_id=1, replica_groups=mesh['bond'=32,'leg'=16] {'bond'}, dimensions={2}, use_global_device_ids=true | all-gather | bytes 540672 | tf_op jit(solution)/shard_map/all_gather | solution.py:40
  271.7 0.3 copy.10
  272.1 1.0 convolution_bitcast_fusion
  273.0 0.6 fusion.6
  273.6 0.6 fusion.5
  274.3 0.6 fusion.1
  274.9 0.6 fusion
  275.6 0.1 pad_maximum_fusion
  275.7 7.0 %convolution_bitcast_fusion.2 = f32[2,8,4,2]{1,2,3,0:T(4,128)S(1)} fusion(f32[2,8,2,64,64]{4,3,2,1,0:T(8,128)S(1)} %pad_maximum_fusion, f32[4,64,64,1,1]{2,1,0,4,3:T(8,128)S(1)} %bitcast.52), kind=kOutput, calls=%fused_computation.6 | convolution fusion | flops 6291456 | bytes 590336 | tf_op jit(solution)/shard_map/pjk,ztqjk->ztpq/dot_general | solution.py:30
  282.7 0.6 copy.13
  (1 shorter events, 0.0 us)
Async XLA Ops:
  3.4 11.4 %copy-start.1 = (f32[2,4096]{1,0:T(2,128)S(1)}, f32[2,4096]{1,0:T(2,128)}, u32[]{:S(2)}) copy-start(f32[2,4096]{1,0:T(2,128)} %param.7) | copy-start | bytes 98308
  3.4 11.5 %copy-start = (f32[4,4096]{1,0:T(4,128)S(1)}, f32[4,4096]{1,0:T(4,128)}, u32[]{:S(2)}) copy-start(f32[4,4096]{1,0:T(4,128)} %param.6) | copy-start | bytes 196612
  3.4 104.6 %all-to-all-start = ((f32[32,64,512]{2,1,0:T(8,128)}), f32[32,64,512]{2,1,0:T(8,128)}, u32[]{:S(2)}, u32[]{:S(2)}) async-start(f32[32,64,512]{2,1,0:T(8,128)} %stack.8), calls=%async_computation | async-start | bytes 8388608 | tf_op jit(solution)/shard_map/all_to_all | solution.py:11
